TPU v7x, 512 devices: a whole 4x4x16 slice. The times are simulated.
512 devices in a mesh: gx: 8 (over z_lo), gy: 8 (over y, z_hi), gz: 8 (over x, core).
Axes of the slice: x: 4, y: 4, z: 16 (z_hi: 2, z_lo: 8; z = z_hi * 8 + z_lo), core: 2. Of those that a mesh axis runs over, the one named last changes fastest.
Arguments:
- state_send: float32 [13, 216, 65536], P(None, None, ('gx', 'gy', 'gz')), may hold values from -0.5 to 14, as said below
- order_send: int32 [65536], P(('gx', 'gy', 'gz')), may hold values from 1 to 5
- send_count: int32 [512, 64], P(('gx', 'gy', 'gz')), may hold values from 0 to 2, as said below
- neighbours: int32 [6, 65536], P(None, ('gx', 'gy', 'gz')), may hold values from 0 to 159, as said below
Outputs:
- new_state: float32 [13, 216, 65536], P(None, None, ('gx', 'gy', 'gz'))
Inputs may be any that keep to these rules, and one draw needn't show every extreme that they name: `state_send`: rows 0 to 8 are species densities in [0.005, 2], rows 9 to 11 momenta in [-0.5, 0.5], row 12 total energy in [3, 14], with energy above 0.5 |momentum|^2 / density at every node. `send_count`: in every draw one receiver of each gx index gets 2 elements from every device of that index. `neighbours`: every face of a live new element names a live element; faces 0, 2, 4 of slots below 16 may name the previous device's last 16 slots, faces 1, 3, 5 of the last 16 slots the next device's first 16; the first device has no previous and the last no next; empty slots name themselves.
All inputs are finite; a program needn't handle non-finite values.
Results may differ from a plain program's by a relative error of at most 0.0003.
Values sent between devices are 32-bit elements; how exact they have to be, the bound alone decides.
No kernel may reach another device: no remote copies, remote signals or barrier semaphores. Data moves between devices by JAX's collectives and lax.ppermute only.
A program may use at most 128 MiB of HBM per device.

v0:
```python
import jax
import jax.numpy as jnp
import numpy as np
from jax import lax
from jax.sharding import PartitionSpec as P

NV = 13
PMAX = 5
NODES = 216
BAND = 16


step_scale = 0.02
positivity_eps = 0.001
floor_gap = 0.05


def padded(value, sides, width):
    for axis, dim in sides:
        count, length = (lax.axis_size(axis), value.shape[dim])
        up = [(i, (i + 1) % count) for i in range(count - 1)]
        down = [(j, i) for i, j in up]
        last = lax.slice_in_dim(value, length - width, length, axis=dim)
        initial = lax.slice_in_dim(value, 0, width, axis=dim)
        before = lax.ppermute(last, axis, up)
        after = lax.ppermute(initial, axis, down)
        value = jnp.concatenate([before, value, after], axis=dim)
    return value


def lagrange_coeffs(node_pos, column):
    coeffs = [1.0]
    denom = 1.0
    for other in range(len(node_pos)):
        if other == column:
            continue
        shifted = [0.0] * (len(coeffs) + 1)
        for power in range(len(coeffs)):
            shifted[power + 1] += coeffs[power]
            shifted[power] -= float(node_pos[other]) * coeffs[power]
        coeffs = shifted
        denom = denom * (float(node_pos[column]) - float(node_pos[other]))
    return [value / denom for value in coeffs]


def poly_value(coeffs, point):
    total = 0.0
    for power in range(len(coeffs)):
        total += coeffs[power] * point**power
    return total


def poly_slope(coeffs, point):
    total = 0.0
    for power in range(1, len(coeffs)):
        total += power * coeffs[power] * point ** (power - 1)
    return total


def poly_integral(coeffs):
    total = 0.0
    for power in range(len(coeffs)):
        total += coeffs[power] * (1.0 - (-1.0) ** (power + 1)) / (power + 1)
    return total


def basis_tables():
    points = PMAX + 1
    common = np.linspace(-1.0, 1.0, points)
    derivs = np.zeros((PMAX, points, points))
    weights = np.zeros((PMAX, points))
    inverse = np.zeros((PMAX, points))
    interp = np.zeros((PMAX, points, points))
    for degree in range(1, PMAX + 1):
        node_pos = np.linspace(-1.0, 1.0, degree + 1)
        for column in range(degree + 1):
            coeffs = lagrange_coeffs(node_pos, column)
            weights[degree - 1, column] = poly_integral(coeffs)
            for row in range(points):
                interp[degree - 1, row, column] = poly_value(coeffs, float(common[row]))
            for row in range(degree + 1):
                derivs[degree - 1, row, column] = poly_slope(coeffs, float(node_pos[row]))
        inverse[degree - 1, : degree + 1] = 1.0 / weights[degree - 1, : degree + 1]
    return (derivs, weights, inverse, interp, weights[PMAX - 1].copy())


def selections(degree):
    points = PMAX + 1
    derivs, weights, inverse, interp, common_w = basis_tables()
    highest = lax.Precision.HIGHEST
    levels = jnp.arange(1, PMAX + 1, dtype=jnp.int32)
    onehot = (degree[None, :] == levels[:, None]).astype(jnp.float32)
    deriv_sel = jnp.einsum(
        "pij,pe->ije", jnp.asarray(derivs, jnp.float32), onehot, precision=highest
    )
    weight_sel = jnp.einsum(
        "pi,pe->ie", jnp.asarray(weights, jnp.float32), onehot, precision=highest
    )
    inverse_sel = jnp.einsum(
        "pi,pe->ie", jnp.asarray(inverse, jnp.float32), onehot, precision=highest
    )
    interp_sel = jnp.einsum(
        "pqj,pe->qje", jnp.asarray(interp, jnp.float32), onehot, precision=highest
    )
    weighted_interp = interp_sel * jnp.asarray(common_w, jnp.float32)[:, None, None]
    positions = jnp.arange(points, dtype=jnp.int32)[:, None]
    is_live = degree[None, :] > 0
    active = ((positions <= degree[None, :]) & is_live).astype(jnp.float32)
    low_sel = ((positions == 0) & is_live).astype(jnp.float32)
    high_sel = ((positions == degree[None, :]) & is_live).astype(jnp.float32)
    return (
        deriv_sel,
        weight_sel,
        inverse_sel,
        interp_sel,
        weighted_interp,
        active,
        low_sel,
        high_sel,
    )


def apply_along(matrix, data, axis):
    total = None
    for column in range(matrix.shape[1]):
        piece = lax.index_in_dim(data, column, axis, keepdims=True)
        shape = [1] * data.ndim
        shape[axis] = matrix.shape[0]
        shape[-1] = matrix.shape[-1]
        term = matrix[:, column, :].reshape(shape) * piece
        total = term if total is None else total + term
    return total


def pick_layer(selector, data, axis):
    total = None
    for row in range(selector.shape[0]):
        piece = lax.index_in_dim(data, row, axis, keepdims=False)
        shape = [1] * piece.ndim
        shape[-1] = selector.shape[-1]
        term = selector[row].reshape(shape) * piece
        total = term if total is None else total + term
    return total


def place_layer(selector, layer, axis):
    expanded = jnp.expand_dims(layer, axis)
    shape = [1] * expanded.ndim
    shape[axis] = selector.shape[0]
    shape[-1] = selector.shape[-1]
    return selector.reshape(shape) * expanded


def element_terms(state_rows, setup):
    deriv_sel, weight_sel, inverse_sel, interp_sel, weighted_interp, active, low_sel, high_sel = (
        setup
    )
    points = PMAX + 1
    slot_count = state_rows.shape[-1]
    node_mask = active[:, None, None, :] * active[None, :, None, :] * active[None, None, :, :]
    field = state_rows.reshape(NV, points, points, points, slot_count) * node_mask[None]
    species = field[:9]
    momentum = field[9:12]
    energy = field[12]
    density = jnp.sum(species, axis=0)
    safe_rho = jnp.where(node_mask > 0, density, 1.0)
    velocity = momentum / safe_rho[None]
    pressure = 0.4 * (energy - 0.5 * jnp.sum(momentum * velocity, axis=0))
    sound_speed = jnp.sqrt(1.4 * jnp.where(node_mask > 0, pressure, 1.0) / safe_rho)
    volume = jnp.zeros_like(field)
    face_list = []
    for axis_pos in range(3):
        normal_vel = velocity[axis_pos]
        unit = jnp.eye(3, dtype=jnp.float32)[axis_pos].reshape(3, 1, 1, 1, 1)
        flux_dim = (
            jnp.concatenate(
                [
                    species * normal_vel[None],
                    momentum * normal_vel[None] + pressure[None] * unit,
                    ((energy + pressure) * normal_vel)[None],
                ],
                axis=0,
            )
            * node_mask[None]
        )
        speeds = (jnp.abs(normal_vel) + sound_speed) * node_mask
        volume = volume + apply_along(deriv_sel, flux_dim, axis_pos + 1)
        for face_side in range(2):
            selector = low_sel if face_side == 0 else high_sel
            normal_sign = -1.0 if face_side == 0 else 1.0
            u_face = pick_layer(selector, field, axis_pos + 1)
            g_face = normal_sign * pick_layer(selector, flux_dim, axis_pos + 1)
            s_face = pick_layer(selector, speeds, axis_pos)
            face_speed = jnp.max(s_face, axis=(0, 1))
            u_common = apply_along(interp_sel, apply_along(interp_sel, u_face, 1), 2)
            g_common = apply_along(interp_sel, apply_along(interp_sel, g_face, 1), 2)
            face_rows = jnp.concatenate(
                [
                    u_common.reshape(NV, points * points, slot_count),
                    g_common.reshape(NV, points * points, slot_count),
                    jnp.broadcast_to(face_speed[None, None, :], (1, points * points, slot_count)),
                ],
                axis=0,
            )
            face_list.append(face_rows)
    traces = jnp.stack(face_list, axis=1)
    return (field, volume, traces, node_mask)


def finish(field, volume, traces, extended, links, setup, node_mask):
    deriv_sel, weight_sel, inverse_sel, interp_sel, weighted_interp, active, low_sel, high_sel = (
        setup
    )
    points = PMAX + 1
    slot_count = field.shape[-1]
    lift_table = weighted_interp.transpose(1, 0, 2)
    surface = jnp.zeros_like(field)
    for face in range(6):
        axis_pos = face // 2
        selector = low_sel if face % 2 == 0 else high_sel
        own_rows = traces[:, face]
        far_rows = jnp.take(extended[:, face ^ 1], links[face], axis=-1)
        penalty = jnp.maximum(own_rows[2 * NV], far_rows[2 * NV])
        jump_flux = 0.5 * (-far_rows[NV : 2 * NV] - own_rows[NV : 2 * NV]) - 0.5 * penalty[None] * (
            far_rows[:NV] - own_rows[:NV]
        )
        jump_flux = jump_flux.reshape(NV, points, points, slot_count)
        inv_face = jnp.sum(selector * inverse_sel, axis=0)
        lifted = apply_along(lift_table, apply_along(lift_table, jump_flux, 1), 2)
        lifted = lifted * (
            inverse_sel[None, :, None, :]
            * inverse_sel[None, None, :, :]
            * inv_face[None, None, None, :]
        )
        surface = surface + place_layer(selector, lifted, axis_pos + 1)
    section = (field - step_scale * (volume + surface)) * node_mask[None]
    node_weight = (
        weight_sel[:, None, None, :]
        * weight_sel[None, :, None, :]
        * weight_sel[None, None, :, :]
        / 8.0
    )
    species = section[:9]
    average = jnp.sum(species * node_weight[None], axis=(1, 2, 3))
    lowest = jnp.min(jnp.where(node_mask[None] > 0, species, 1e30), axis=(1, 2, 3))
    scaling = jnp.minimum(
        1.0, jnp.maximum(average - positivity_eps, 0.0) / jnp.maximum(average - lowest, floor_gap)
    )
    scaled = (
        average[:, None, None, None, :]
        + scaling[:, None, None, None, :] * (species - average[:, None, None, None, :])
    ) * node_mask[None]
    return jnp.concatenate([scaled, section[9:]], axis=0).reshape(NV, NODES, slot_count)


def local(state_send, order_send, send_count, neighbours):
    slot_count = state_send.shape[-1]
    peer_count = lax.axis_size(("gy", "gz"))
    capacity = slot_count // peer_count
    positions = jnp.arange(slot_count, dtype=jnp.int32)
    per_slot = jnp.broadcast_to(send_count.reshape(peer_count, 1), (peer_count, capacity)).reshape(
        slot_count
    )
    live_send = positions % capacity < per_slot
    order_tags = jnp.where(live_send, order_send, 0).astype(jnp.float32).reshape(1, 1, slot_count)
    moved, tags_in = (
        lax.all_to_all(state_send, ("gy", "gz"), split_axis=2, concat_axis=2, tiled=True),
        lax.all_to_all(order_tags, ("gy", "gz"), split_axis=2, concat_axis=2, tiled=True),
    )
    degree = tags_in.reshape(slot_count).astype(jnp.int32)
    setup = selections(degree)
    field, volume, traces, node_mask = element_terms(moved, setup)
    extended = padded(traces, ((("gx", "gy", "gz"), 3),), BAND)
    return finish(field, volume, traces, extended, neighbours, setup, node_mask)


def solution(mesh):
    placed = (
        P(None, None, ("gx", "gy", "gz")),
        P(("gx", "gy", "gz")),
        P(("gx", "gy", "gz"), None),
        P(None, ("gx", "gy", "gz")),
    )
    return jax.shard_map(
        local,
        mesh=mesh,
        in_specs=placed,
        out_specs=P(None, None, ("gx", "gy", "gz")),
        check_vma=False,
    )
```

profile of v0, /device:TPU:32, one launch (start us, length us, event | category | flops | bytes accessed | tf_op | source)
XLA Modules:
  0.0 377.5 jit_solution(7790423187221642835)
XLA Ops:
  2.3 20.3 %all-to-all-start.1 = ((f32[1,1,128]{1,0,2:T(1,128)}), f32[1,1,128]{1,0,2:T(1,128)S(1)}, u32[]{:S(2)}, u32[]{:S(2)}) async-start(f32[1,1,128]{1,0,2:T(1,128)} %copy.2597), calls=%async_computation.1 | async-start | bytes 131072 | tf_op jit(solution)/shard_map/all_to_all | solution.py:268
  25.3 3.0 copy.2595
  28.3 11.0 %all-to-all-done.1 = f32[1,1,128]{1,0,2:T(1,128)S(1)} async-done(((f32[1,1,128]{1,0,2:T(1,128)}), f32[1,1,128]{1,0,2:T(1,128)S(1)}, u32[]{:S(2)}, u32[]{:S(2)}) %all-to-all-start.1) | async-done | bytes 544 | tf_op jit(solution)/shard_map/all_to_all | solution.py:268
  39.3 6.7 %all-to-all-start = ((f32[13,216,128]{1,0,2:T(8,128)}), f32[13,216,128]{1,0,2:T(8,128)S(1)}, u32[]{:S(2)}, u32[]{:S(2)}) async-start(f32[13,216,128]{1,0,2:T(8,128)} %copy.2595), calls=%async_computation | async-start | bytes 4194304 | tf_op jit(solution)/shard_map/all_to_all | solution.py:267
  47.3 2.4 convert_reduce_fusion
  61.4 89.4 %all-to-all-done = f32[13,216,128]{1,0,2:T(8,128)S(1)} async-done(((f32[13,216,128]{1,0,2:T(8,128)}), f32[13,216,128]{1,0,2:T(8,128)S(1)}, u32[]{:S(2)}, u32[]{:S(2)}) %all-to-all-start) | async-done | bytes 1437728 | tf_op jit(solution)/shard_map/all_to_all | solution.py:267
  178.0 3.9 %fusion.139 = (f32[27,6,36,16]{3,2,0,1:T(8,128)}, f32[27,6,36,16]{3,2,0,1:T(8,128)}) fusion(f32[27,6,36,128]{3,2,0,1:T(8,128)S(1)} %fusion.5), kind=kLoop, calls=%fused_computation.678 | loop fusion | bytes 1492992 | tf_op jit(solution)/shard_map/slice | solution.py:23
  181.9 3.5 copy.2746
  185.4 2.4 collective-permute-start
  187.8 3.5 copy.2747
  191.4 15.3 %collective-permute-start.1 = (f32[27,6,36,16]{2,3,1,0:T(8,128)}, f32[27,6,36,16]{2,3,1,0:T(8,128)}, u32[]{:S(2)}, u32[]{:S(2)}) collective-permute-start(f32[27,6,36,16]{2,3,1,0:T(8,128)} %copy.2747), channel_id=1, source_target_pairs={{1,0},{2,1},{3,2},{4,3},{5,4},{6,5},{7,6},{8,7},{9,8},{10,9},{11,1... | collective-permute-start | bytes 1119752 | tf_op jit(solution)/shard_map/ppermute | solution.py:26
  215.5 62.9 %collective-permute-done = f32[27,6,36,16]{2,3,1,0:T(8,128)} collective-permute-done((f32[27,6,36,16]{2,3,1,0:T(8,128)}, f32[27,6,36,16]{2,3,1,0:T(8,128)}, u32[]{:S(2)}, u32[]{:S(2)}) %collective-permute-start) | collective-permute-done | bytes 373280 | tf_op jit(solution)/shard_map/ppermute | solution.py:25
  278.3 3.8 %copy.2748 = f32[27,6,36,16]{3,2,0,1:T(8,128)} copy(f32[27,6,36,16]{2,3,1,0:T(8,128)} %collective-permute-done) | data formatting | bytes 746496 | tf_op jit(solution)/shard_map/ppermute | solution.py:25
  282.2 3.6 copy.2749
  285.8 5.6 %pad_maximum_fusion = f32[27,6,36,160]{3,2,0,1:T(8,128)S(1)} fusion(f32[27,6,36,16]{3,2,0,1:T(8,128)} %copy.2749, f32[27,6,36,128]{3,2,0,1:T(8,128)S(1)} %fusion.5, f32[27,6,36,16]{3,2,0,1:T(8,128)} %copy.2748), kind=kLoop, calls=%fused_computation.6 | loop fusion | flops 1866240 | bytes 7464960 | tf_op jit(solution)/shard_map/concatenate | solution.py:27
  293.3 3.4 copy.2762
  296.7 3.9 %gather_fusion.3 = f32[128,27,36]{2,1,0:T(8,128)} fusion(f32[27,36,160]{1,0,2:T(8,128)} %copy.2762, s32[1024]{0:T(1024)} %get-tuple-element.415), kind=kCustom, calls=%fused_computation.3.clone | custom fusion | bytes 995840 | tf_op jit(solution)/shard_map/jit(_take)/gather | solution.py:222
  300.6 3.3 copy.2763
  306.9 3.4 copy.2758
  310.3 3.9 %gather_fusion.2 = f32[128,27,36]{2,1,0:T(8,128)} fusion(f32[27,36,160]{1,0,2:T(8,128)} %copy.2758, s32[1024]{0:T(1024)} %get-tuple-element.416), kind=kCustom, calls=%fused_computation.2.clone | custom fusion | bytes 995840 | tf_op jit(solution)/shard_map/jit(_take)/gather | solution.py:222
  314.2 3.3 copy.2759
  321.7 3.4 copy.2754
  325.1 3.9 %gather_fusion.1 = f32[128,27,36]{2,1,0:T(8,128)} fusion(f32[27,36,160]{1,0,2:T(8,128)} %copy.2754, s32[1024]{0:T(1024)} %get-tuple-element.417), kind=kCustom, calls=%fused_computation.1.clone | custom fusion | bytes 995840 | tf_op jit(solution)/shard_map/jit(_take)/gather | solution.py:222
  328.9 3.3 copy.2755
  335.2 2.6 copy.2750
  337.8 3.9 %gather_fusion = f32[128,27,36]{2,1,0:T(8,128)} fusion(f32[27,36,160]{1,0,2:T(8,128)} %copy.2750, s32[1024]{0:T(1024)} %get-tuple-element.418), kind=kCustom, calls=%fused_computation.clone | custom fusion | bytes 995840 | tf_op jit(solution)/shard_map/jit(_take)/gather | solution.py:222
  341.7 2.6 copy.2751
  347.6 2.8 copy.2769
  350.4 2.5 gather_fusion.5
  357.9 2.6 copy.2766
  360.5 2.5 gather_fusion.4
  368.9 4.9 %subtract_multiply_fusion = f32[13,6,6,6,128]{4,0,2,1,3:T(8,128)S(1)} fusion(f32[13,6,6,128]{3,0,2,1:T(8,128)S(1)} %add_multiply_fusion.1, f32[6,128]{1,0:T(8,128)S(1)} %copy-done.114, f32[13,6,6,128]{3,0,2,1:T(8,128)S(1)} %add_multiply_fusion.2, f32[6,128]{1,0:T(8,128)} %copy-done.115, f32[13,6,6,128]{3,0,2,1:T(8,128)S(1)} %copy-done.7, ...), kind=kLoop, calls=%fused_computation.16 | loop fusion | flops 18330624 | bytes 8761344 | tf_op jit(solution)/shard_map/mul | solution.py:236
  (578 shorter events, 80.4 us)
Async XLA Ops:
  2.3 37.0 %all-to-all-start.1 = ((f32[1,1,128]{1,0,2:T(1,128)}), f32[1,1,128]{1,0,2:T(1,128)S(1)}, u32[]{:S(2)}, u32[]{:S(2)}) async-start(f32[1,1,128]{1,0,2:T(1,128)} %copy.2597), calls=%async_computation.1 | async-start | bytes 131072 | tf_op jit(solution)/shard_map/all_to_all | solution.py:268
  28.3 22.8 %copy-start.152 = (f32[5,6,6]{0,2,1:T(8,128)S(1)}, f32[5,6,6]{0,2,1:T(8,128)}, u32[]{:S(2)}) copy-start(f32[5,6,6]{0,2,1:T(8,128)} %constant.79.clone) | copy-start | bytes 2164
  28.3 27.9 %copy-start.154 = (f32[5,6]{1,0:T(8,128)S(1)}, f32[5,6]{1,0:T(8,128)}, u32[]{:S(2)}) copy-start(f32[5,6]{1,0:T(8,128)} %constant.77.clone) | copy-start | bytes 364
  28.3 28.1 %copy-start.153 = (f32[5,6]{1,0:T(8,128)S(1)}, f32[5,6]{1,0:T(8,128)}, u32[]{:S(2)}) copy-start(f32[5,6]{1,0:T(8,128)} %constant.78.clone) | copy-start | bytes 364
  28.3 28.3 %copy-start.151 = (f32[5,6,6]{0,2,1:T(8,128)S(1)}, f32[5,6,6]{0,2,1:T(8,128)}, u32[]{:S(2)}) copy-start(f32[5,6,6]{0,2,1:T(8,128)} %constant.76.clone) | copy-start | bytes 2164
  28.3 30.4 %copy-start.150 = (f32[6]{0:T(128)S(1)}, f32[6]{0:T(128)}, u32[]{:S(2)}) copy-start(f32[6]{0:T(128)} %constant.80.clone) | copy-start | bytes 76
  39.3 111.5 %all-to-all-start = ((f32[13,216,128]{1,0,2:T(8,128)}), f32[13,216,128]{1,0,2:T(8,128)S(1)}, u32[]{:S(2)}, u32[]{:S(2)}) async-start(f32[13,216,128]{1,0,2:T(8,128)} %copy.2595), calls=%async_computation | async-start | bytes 4194304 | tf_op jit(solution)/shard_map/all_to_all | solution.py:267
  49.7 11.6 %copy-start.62 = (f32[6,128]{1,0:T(8,128)}, f32[6,128]{1,0:T(8,128)S(1)}, u32[]{:S(2)}) copy-start(f32[6,128]{1,0:T(8,128)S(1)} %get-tuple-element.390) | copy-start | bytes 9220
  49.7 11.6 %copy-start.113 = (f32[6,128]{1,0:T(8,128)}, f32[6,128]{1,0:T(8,128)S(1)}, u32[]{:S(2)}) copy-start(f32[6,128]{1,0:T(8,128)S(1)} %get-tuple-element.389) | copy-start | bytes 9220
  49.7 11.6 %copy-start.115 = (f32[6,128]{1,0:T(8,128)}, f32[6,128]{1,0:T(8,128)S(1)}, u32[]{:S(2)}) copy-start(f32[6,128]{1,0:T(8,128)S(1)} %get-tuple-element.392) | copy-start | bytes 9220
  49.7 11.6 %copy-start.41 = (f32[6,6,128]{2,1,0:T(8,128)}, f32[6,6,128]{2,1,0:T(8,128)S(1)}, u32[]{:S(2)}) copy-start(f32[6,6,128]{2,1,0:T(8,128)S(1)} %broadcast_multiply_fusion.2) | copy-start | bytes 55300
  51.4 10.0 %copy-start.70 = (f32[6,128]{1,0:T(8,128)}, f32[6,128]{1,0:T(8,128)S(1)}, u32[]{:S(2)}) copy-start(f32[6,128]{1,0:T(8,128)S(1)} %get-tuple-element.399) | copy-start | bytes 9220
  52.6 8.8 %copy-start.74 = (f32[6,128]{1,0:T(8,128)}, f32[6,128]{1,0:T(8,128)S(1)}, u32[]{:S(2)}) copy-start(f32[6,128]{1,0:T(8,128)S(1)} %get-tuple-element.397) | copy-start | bytes 9220
  52.6 8.8 %copy-start.76 = (f32[6,128]{1,0:T(8,128)}, f32[6,128]{1,0:T(8,128)S(1)}, u32[]{:S(2)}) copy-start(f32[6,128]{1,0:T(8,128)S(1)} %get-tuple-element.398) | copy-start | bytes 9220
  53.8 7.6 %copy-start.78 = (f32[6,128]{1,0:T(8,128)}, f32[6,128]{1,0:T(8,128)S(1)}, u32[]{:S(2)}) copy-start(f32[6,128]{1,0:T(8,128)S(1)} %get-tuple-element.395) | copy-start | bytes 9220
  53.8 7.6 %copy-start.80 = (f32[6,128]{1,0:T(8,128)}, f32[6,128]{1,0:T(8,128)S(1)}, u32[]{:S(2)}) copy-start(f32[6,128]{1,0:T(8,128)S(1)} %get-tuple-element.396) | copy-start | bytes 9220
  162.4 8.9 %copy-start.134 = (f32[128]{0:T(128)}, f32[128]{0:T(128)S(1)}, u32[]{:S(2)}) copy-start(f32[128]{0:T(128)S(1)} %add_reduce_fusion.5) | copy-start | bytes 1540
  162.5 11.7 %copy-start.136 = (f32[128]{0:T(128)}, f32[128]{0:T(128)S(1)}, u32[]{:S(2)}) copy-start(f32[128]{0:T(128)S(1)} %add_reduce_fusion.4) | copy-start | bytes 1540
  162.6 14.6 %copy-start.138 = (f32[128]{0:T(128)}, f32[128]{0:T(128)S(1)}, u32[]{:S(2)}) copy-start(f32[128]{0:T(128)S(1)} %get-tuple-element.13) | copy-start | bytes 1540
  162.6 14.7 %copy-start.130 = (f32[128]{0:T(128)}, f32[128]{0:T(128)S(1)}, u32[]{:S(2)}) copy-start(f32[128]{0:T(128)S(1)} %get-tuple-element.12) | copy-start | bytes 1540
  162.7 14.6 %copy-start.140 = (f32[128]{0:T(128)}, f32[128]{0:T(128)S(1)}, u32[]{:S(2)}) copy-start(f32[128]{0:T(128)S(1)} %get-tuple-element.11) | copy-start | bytes 1540
  162.7 14.7 %copy-start.132 = (f32[128]{0:T(128)}, f32[128]{0:T(128)S(1)}, u32[]{:S(2)}) copy-start(f32[128]{0:T(128)S(1)} %get-tuple-element.10) | copy-start | bytes 1540
  169.9 7.9 %copy-start.22 = (f32[13,36,128]{2,1,0:T(8,128)}, f32[13,36,128]{2,1,0:T(8,128)S(1)}, u32[]{:S(2)}) copy-start(f32[13,36,128]{2,1,0:T(8,128)S(1)} %get-tuple-element.317) | copy-start | bytes 718852
  185.4 92.9 %collective-permute-start = (f32[27,6,36,16]{2,3,1,0:T(8,128)}, f32[27,6,36,16]{2,3,1,0:T(8,128)}, u32[]{:S(2)}, u32[]{:S(2)}) collective-permute-start(f32[27,6,36,16]{2,3,1,0:T(8,128)} %copy.2746), channel_id=1, source_target_pairs={{0,1},{1,2},{2,3},{3,4},{4,5},{5,6},{6,7},{7,8},{8,9},{9,10},{10,1... | collective-permute-start | bytes 1119752 | tf_op jit(solution)/shard_map/ppermute | solution.py:25
  187.8 18.9 %copy-start.128 = (f32[6,1,128]{2,1,0:T(1,128)S(1)}, f32[6,1,128]{2,1,0:T(1,128)}, u32[]{:S(2)}) copy-start(f32[6,1,128]{2,1,0:T(1,128)} %get-tuple-element.322) | copy-start | bytes 9220
  187.8 18.9 %copy-start.129 = (f32[6,1,128]{2,1,0:T(1,128)S(1)}, f32[6,1,128]{2,1,0:T(1,128)}, u32[]{:S(2)}) copy-start(f32[6,1,128]{2,1,0:T(1,128)} %get-tuple-element.327) | copy-start | bytes 9220
  187.8 18.9 %copy-start.111 = (pred[6,6,6,128]{3,2,1,0:T(8,128)(4,1)S(1)}, pred[6,6,6,128]{3,2,1,0:T(8,128)(4,1)}, u32[]{:S(2)}) copy-start(pred[6,6,6,128]{3,2,1,0:T(8,128)(4,1)} %multiply_compare_fusion) | copy-start | bytes 82948
  191.4 22.9 %copy-start.1 = (f32[13,6,6,6,128]{4,0,2,1,3:T(8,128)S(1)}, f32[13,6,6,6,128]{4,0,2,1,3:T(8,128)}, u32[]{:S(2)}) copy-start(f32[13,6,6,6,128]{4,0,2,1,3:T(8,128)} %copy-done) | copy-start | bytes 4313092
  191.4 90.8 %collective-permute-start.1 = (f32[27,6,36,16]{2,3,1,0:T(8,128)}, f32[27,6,36,16]{2,3,1,0:T(8,128)}, u32[]{:S(2)}, u32[]{:S(2)}) collective-permute-start(f32[27,6,36,16]{2,3,1,0:T(8,128)} %copy.2747), channel_id=1, source_target_pairs={{1,0},{2,1},{3,2},{4,3},{5,4},{6,5},{7,6},{8,7},{9,8},{10,9},{11,1... | collective-permute-start | bytes 1119752 | tf_op jit(solution)/shard_map/ppermute | solution.py:26
  296.7 7.2 %copy-start.146 = (pred[128]{0:T(512)(128)(4,1)S(1)}, pred[128]{0:T(512)(128)(4,1)}, u32[]{:S(2)}) copy-start(pred[128]{0:T(512)(128)(4,1)} %get-tuple-element.360) | copy-start | bytes 388
  310.3 7.2 %copy-start.145 = (pred[128]{0:T(512)(128)(4,1)S(1)}, pred[128]{0:T(512)(128)(4,1)}, u32[]{:S(2)}) copy-start(pred[128]{0:T(512)(128)(4,1)} %get-tuple-element.362) | copy-start | bytes 388
  325.1 7.2 %copy-start.144 = (pred[128]{0:T(512)(128)(4,1)S(1)}, pred[128]{0:T(512)(128)(4,1)}, u32[]{:S(2)}) copy-start(pred[128]{0:T(512)(128)(4,1)} %get-tuple-element.364) | copy-start | bytes 388
  (127 other events, 256.8 us)
where the time goes:
time: 383 us; the launch traced here: 378 us
  waiting for transfers between devices  163 us (43%)
  local copies, waits for them, and re-layouts  119 us (31%)
  other arithmetic  46.5 us (12%)
  starting transfers between devices  44.7 us (12%)
    all_to_all x1, waiting for transfers between devices, local(): lax.all_to_all(state_send, ('gy', 'gz'), split_axis=2, concat_axis=2, til...  89.4 us
    ppermute x1, waiting for transfers between devices, padded(): before = lax.ppermute(last, axis, up)  62.9 us
    gather x12, local copies, waits for them, and re-layouts, finish(): far_rows = jnp.take(extended[:, face ^ 1], links[face], axis=-1)  36.2 us
    all_to_all x1, starting transfers between devices, local(): lax.all_to_all(order_tags, ('gy', 'gz'), split_axis=2, concat_axis=2, til...  20.3 us
    squeeze x7, local copies, waits for them, and re-layouts, finish(): far_rows = jnp.take(extended[:, face ^ 1], links[face], axis=-1)  20.2 us
    unnamed x322, local copies, waits for them, and re-layouts  19.7 us
    ppermute x1, starting transfers between devices, padded(): after = lax.ppermute(initial, axis, down)  15.3 us
    mul x122, local copies, waits for them, and re-layouts, apply_along(): term = matrix[:, column, :].reshape(shape) * piece  13.3 us
  transfers between devices with their start and end apart: 4, of which 3 were waited for; matrix products, arithmetic and copies ran while one was open for 9% of the time, Pallas kernels for 0%

commit v1 on v0

v1 whole, which is shorter than its diff:
```python
import jax
import jax.numpy as jnp
import numpy as np
from jax import lax
from jax.experimental import pallas as pl
from jax.experimental.pallas import tpu as pltpu
from jax.sharding import PartitionSpec as P

NV = 13
PMAX = 5
PTS = PMAX + 1
NODES = 216
FACE = 36
BAND = 16
SLOTS = 128
ROWS = 22
PITCH = 24
FEATS = ROWS * 128
HALO = 216

step_scale = 0.02
positivity_eps = 0.001
floor_gap = 0.05

AXES = ("gx", "gy", "gz")
GROUP = ("gy", "gz")
D0, M1, M2, W0, ACT, OWN_ROWS = 0, 40, 80, 120, 128, 136


def lagrange_coeffs(node_pos, column):
    coeffs = [1.0]
    denom = 1.0
    for other in range(len(node_pos)):
        if other == column:
            continue
        shifted = [0.0] * (len(coeffs) + 1)
        for power in range(len(coeffs)):
            shifted[power + 1] += coeffs[power]
            shifted[power] -= float(node_pos[other]) * coeffs[power]
        coeffs = shifted
        denom = denom * (float(node_pos[column]) - float(node_pos[other]))
    return [value / denom for value in coeffs]


def poly_value(coeffs, point):
    total = 0.0
    for power in range(len(coeffs)):
        total += coeffs[power] * point**power
    return total


def poly_slope(coeffs, point):
    total = 0.0
    for power in range(1, len(coeffs)):
        total += power * coeffs[power] * point ** (power - 1)
    return total


def poly_integral(coeffs):
    total = 0.0
    for power in range(len(coeffs)):
        total += coeffs[power] * (1.0 - (-1.0) ** (power + 1)) / (power + 1)
    return total


def basis_tables():
    points = PMAX + 1
    common = np.linspace(-1.0, 1.0, points)
    derivs = np.zeros((PMAX, points, points))
    weights = np.zeros((PMAX, points))
    inverse = np.zeros((PMAX, points))
    interp = np.zeros((PMAX, points, points))
    for degree in range(1, PMAX + 1):
        node_pos = np.linspace(-1.0, 1.0, degree + 1)
        for column in range(degree + 1):
            coeffs = lagrange_coeffs(node_pos, column)
            weights[degree - 1, column] = poly_integral(coeffs)
            for row in range(points):
                interp[degree - 1, row, column] = poly_value(coeffs, float(common[row]))
            for row in range(degree + 1):
                derivs[degree - 1, row, column] = poly_slope(coeffs, float(node_pos[row]))
        inverse[degree - 1, : degree + 1] = 1.0 / weights[degree - 1, : degree + 1]
    return (derivs, weights, inverse, interp, weights[PMAX - 1].copy())


def shell_order():
    nodes = [(a, b, c) for a in range(PTS) for b in range(PTS) for c in range(PTS)]
    ranked = sorted(range(NODES), key=lambda n: (max(1, *nodes[n]), n))
    rank = [0] * NODES
    for r, n in enumerate(ranked):
        rank[n] = r
    return rank, [max(1, *abc) for abc in nodes]


RANK, LEVEL = shell_order()


def element_tables():
    derivs, weights, inverse, interp, common = basis_tables()
    own = np.zeros((OWN_ROWS, 128))
    far = np.zeros((80, 128))
    for p in range(1, PMAX + 1):
        deriv, weight, inv, value = (derivs[p - 1], weights[p - 1], inverse[p - 1], interp[p - 1])
        own[D0 : D0 + 36, p] = -step_scale * deriv.reshape(36)
        lift = inv[:, None] * value.T * common[None, :]
        both = lift @ value
        own[M1 : M1 + 36, p] = both.reshape(36)
        own[M2 : M2 + 36, p] = step_scale * inv[0] * both.reshape(36)
        own[W0 : W0 + 6, p] = 0.5 * weight
        own[ACT : ACT + p + 1, p] = 1.0
        for r in range(1, PMAX + 1):
            both = lift @ interp[r - 1]
            column = (p - 1) * 5 + (r - 1)
            far[0:36, column] = both.reshape(36)
            far[40:76, column] = -step_scale * inv[0] * both.reshape(36)
    return jnp.asarray(own, jnp.float32), jnp.asarray(far, jnp.float32)


def iota(shape, axis):
    return lax.broadcasted_iota(jnp.int32, shape, axis)


def row8(ref, row):
    return jnp.broadcast_to(ref[pl.ds(row, 1), :], (8, SLOTS))


def node_of(axis, layer, b, c):
    if axis == 0:
        return layer * 36 + b * 6 + c
    if axis == 1:
        return b * 36 + layer * 6 + c
    return b * 36 + c * 6 + layer


def block(ref, index, unit=8, offset=0):
    if isinstance(index, int):
        start = index * unit + offset
    else:
        start = pl.multiple_of(index * unit + offset, 8)
    return ref.at[pl.ds(start, 8), :]


def pack_body(peers, state, order, count, out, feats):
    capacity = SLOTS // peers
    spread = (iota((peers, SLOTS), 1) // capacity == iota((peers, SLOTS), 0)).astype(jnp.float32)
    counts = jnp.broadcast_to(count[...].astype(jnp.float32), (8, peers))
    per_slot = jnp.dot(counts, spread, preferred_element_type=jnp.float32)
    place = (iota((8, SLOTS), 1) % capacity).astype(jnp.float32)
    orders = jnp.broadcast_to(order[...].astype(jnp.float32), (8, SLOTS))
    tag = jnp.where(place < per_slot, orders, 0.0)
    for n in range(NODES):
        feats[pl.ds(RANK[n] * NV, NV), :] = state[pl.ds(n, NV, stride=NODES), :]
    feats[pl.ds(NODES * NV, 8), :] = tag
    for k in range(ROWS):
        out[pl.ds(k, SLOTS, stride=PITCH), :] = feats[pl.ds(k * 128, 128), :].T


def pack(state, order, count):
    peers = count.shape[-1]
    return pl.pallas_call(
        lambda *refs: pack_body(peers, *refs),
        out_shape=jax.ShapeDtypeStruct((SLOTS * PITCH, 128), jnp.float32),
        scratch_shapes=[pltpu.VMEM((FEATS, SLOTS), jnp.float32)],
        name="pack",
    )(state, order, count)


def prep_body(recv, own_table, a_ref, b_ref, high, up, down, tab, order, feats):
    for k in range(ROWS):
        feats[pl.ds(k * 128, 128), :] = recv[pl.ds(k, SLOTS, stride=PITCH), :].T
    ob = row8(feats, NODES * NV)
    order[...] = ob
    pick = (iota((128, SLOTS), 0).astype(jnp.float32) == ob[0:1, :]).astype(jnp.float32)
    tab[...] = jnp.dot(
        own_table[...], pick, precision=lax.Precision.HIGHEST, preferred_element_type=jnp.float32
    )
    live = [None] + [ob >= float(m) for m in range(1, PMAX + 1)]
    for n in range(NODES):
        act = live[LEVEL[n]]
        first = RANK[n] * NV
        a_ref[pl.ds(n * 8, 8), :] = jnp.where(act, feats[pl.ds(first, 8), :], 0.0)
        second = jnp.where(act, feats[pl.ds(first + 8, 8), :], 0.0)
        for axis in range(3):
            b_ref[pl.ds((axis * NODES + n) * 8, 8), :] = second
    lane_row = iota((8, SLOTS), 0)

    def primitives(g, carry):
        n = g * 8 + lane_row
        top = jnp.maximum(jnp.maximum(n // 36, (n // 6) % 6), jnp.maximum(n % 6, 1))
        act = ob >= top.astype(jnp.float32)
        base = g * 64
        species = [a_ref[pl.ds(base + v, 8, stride=8), :] for v in range(8)]
        species.append(b_ref[pl.ds(base, 8, stride=8), :])
        momentum = [b_ref[pl.ds(base + 1 + i, 8, stride=8), :] for i in range(3)]
        energy = b_ref[pl.ds(base + 4, 8, stride=8), :]
        rho = species[0]
        for value in species[1:]:
            rho = rho + value
        inv = 1.0 / jnp.where(act, rho, 1.0)
        velocity = [value * inv for value in momentum]
        kinetic = momentum[0] * velocity[0] + momentum[1] * velocity[1] + momentum[2] * velocity[2]
        pressure = 0.4 * (energy - 0.5 * kinetic)
        sound = jnp.sqrt(1.4 * jnp.where(act, pressure, 1.0) * inv)
        for axis in range(3):
            start = axis * NODES * 8 + base
            b_ref[pl.ds(start + 5, 8, stride=8), :] = pressure
            b_ref[pl.ds(start + 6, 8, stride=8), :] = velocity[axis]
            b_ref[pl.ds(start + 7, 8, stride=8), :] = jnp.where(
                act, jnp.abs(velocity[axis]) + sound, 0.0
            )
        return carry

    lax.fori_loop(0, NODES // 8, primitives, 0)
    is_top = [None] + [ob == float(m) for m in range(1, PMAX + 1)]
    lane = iota((8, SLOTS), 1)
    group = lane // BAND
    up_now = down_now = None
    for axis in range(3):
        for q in range(FACE):
            b, c = divmod(q, 6)
            for part in range(2):
                ref = a_ref if part == 0 else b_ref
                shift = 0 if part == 0 else axis * NODES

                def read(layer):
                    return ref[pl.ds((shift + node_of(axis, layer, b, c)) * 8, 8), :]

                top = read(1)
                for m in range(2, PMAX + 1):
                    top = jnp.where(is_top[m], read(m), top)
                index = (axis * FACE + q) * 2 + part
                high[pl.ds(index * 8, 8), :] = top
                word, k = divmod(index, 8)
                moved_up = pltpu.roll(top, (16 * k - (SLOTS - BAND)) % SLOTS, 1)
                low = read(0)
                moved_down = pltpu.roll(low, 16 * k, 1) if k else low
                up_now = moved_up if k == 0 else jnp.where(group == k, moved_up, up_now)
                down_now = moved_down if k == 0 else jnp.where(group == k, moved_down, down_now)
                if k == 7:
                    up[pl.ds(word * 8, 8), :] = up_now
                    down[pl.ds(word * 8, 8), :] = down_now
    up[pl.ds(HALO, 8), :] = pltpu.roll(ob, BAND, 1)
    down[pl.ds(HALO, 8), :] = ob


def prep(recv, own_table):
    shape = lambda rows: jax.ShapeDtypeStruct((rows, SLOTS), jnp.float32)
    return pl.pallas_call(
        prep_body,
        out_shape=(
            shape(NODES * 8),
            shape(3 * NODES * 8),
            shape(3 * FACE * 16),
            shape(HALO + 8),
            shape(HALO + 8),
            shape(OWN_ROWS),
            shape(8),
        ),
        scratch_shapes=[pltpu.VMEM((FEATS, SLOTS), jnp.float32)],
        name="prep",
    )(recv, own_table)


def flux_rows(axis, scale):
    rows = iota((8, SLOTS), 0)
    return (
        jnp.where(rows == 1 + axis, scale, 0.0).astype(jnp.float32),
        jnp.where(rows == 4, scale, 0.0).astype(jnp.float32),
    )


def volume_body(a_ref, b_ref, tab, acc):
    for axis in range(3):
        normal_row, energy_row = flux_rows(axis, 1.0)
        stride = (36, 6, 1)[axis]

        def pencil(t, carry):
            base = (t, (t // 6) * 36 + t % 6, t * 6)[axis]
            flux_a, flux_b = [], []
            for j in range(6):
                n = base + j * stride
                where = pl.multiple_of((axis * NODES + n) * 8, 8)
                speed = row8(b_ref, where + 6)
                pressure = row8(b_ref, where + 5)
                flux_a.append(block(a_ref, n)[...] * speed)
                flux_b.append(
                    b_ref[pl.ds(where, 8), :] * speed
                    + pressure * (normal_row + energy_row * speed)
                )
            for i in range(6):
                n = base + i * stride
                if axis == 0:
                    sum_a = block(a_ref, n)[...]
                    sum_b = block(b_ref, n)[...]
                else:
                    sum_a = block(acc, n, 16)[...]
                    sum_b = block(acc, n, 16, 8)[...]
                for j in range(6):
                    factor = row8(tab, D0 + i * 6 + j)
                    sum_a = sum_a + factor * flux_a[j]
                    sum_b = sum_b + factor * flux_b[j]
                block(acc, n, 16)[...] = sum_a
                block(acc, n, 16, 8)[...] = sum_b
            return carry

        lax.fori_loop(0, FACE, pencil, 0)


def volume(a, b, tab):
    return pl.pallas_call(
        volume_body,
        out_shape=jax.ShapeDtypeStruct((NODES * 16, SLOTS), jnp.float32),
        name="volume",
    )(a, b, tab)


def gather_lanes(value, index):
    return jnp.take_along_axis(value, index, axis=1)


def finish_body(
    a_ref, b_ref, high, acc_in, tab, order, links, before, after, far_table,
    out, acc, far, own_mid, far_mid, pair,
):
    acc[...] = acc_in[...]
    ob = order[...]
    for face in range(6):
        axis, side = divmod(face, 2)
        sign = 0.5 if side else -0.5
        halo = after if side else before
        link = jnp.broadcast_to(links[pl.ds(face, 1), :], (8, SLOTS))
        outside = link >= BAND + SLOTS if side else link < BAND
        halo_lane = jnp.where(outside, link - (BAND + SLOTS if side else 0), 0)
        own_lane = jnp.clip(link - BAND, 0, SLOTS - 1)
        far_order = jnp.where(
            outside,
            gather_lanes(halo[pl.ds(HALO, 8), :], halo_lane),
            gather_lanes(ob, own_lane),
        )
        column = jnp.where(ob > 0.0, (ob - 1.0) * 5.0 + far_order - 1.0, -1.0)
        pick = (iota((128, SLOTS), 0).astype(jnp.float32) == column[0:1, :]).astype(jnp.float32)
        pair[...] = jnp.dot(
            far_table[...],
            pick,
            precision=lax.Precision.HIGHEST,
            preferred_element_type=jnp.float32,
        )

        def low_block(part, q):
            b, c = divmod(q, 6)
            n = node_of(axis, 0, b, c)
            if part == 0:
                return a_ref[pl.ds(n * 8, 8), :]
            return b_ref[pl.ds((axis * NODES + n) * 8, 8), :]

        def high_block(part, q):
            return high[pl.ds(((axis * FACE + q) * 2 + part) * 8, 8), :]

        inner, outer = (high_block, low_block) if side else (low_block, high_block)
        fastest = None
        for q in range(FACE):
            for part in range(2):
                word, k = divmod((axis * FACE + q) * 2 + part, 8)
                here = gather_lanes(outer(part, q), own_lane)
                there = gather_lanes(halo[pl.ds(word * 8, 8), :], halo_lane + 16 * k)
                value = jnp.where(outside, there, here)
                far[pl.ds((q * 2 + part) * 8, 8), :] = value
                if part == 1:
                    value = jnp.maximum(value, inner(1, q))
                    fastest = value if fastest is None else jnp.maximum(fastest, value)
        penalty = 0.5 * jnp.broadcast_to(fastest[7:8, :], (8, SLOTS))
        normal_row, energy_row = flux_rows(axis, sign)

        def weighted(block_a, ref_b, start):
            start = pl.multiple_of(start, 8)
            speed = row8(ref_b, start + 6)
            pressure = row8(ref_b, start + 5)
            mix = sign * speed - penalty
            return (
                block_a * mix,
                ref_b[pl.ds(start, 8), :] * mix + pressure * (normal_row + energy_row * speed),
            )

        def first(k, carry):
            for ours in (True, False):
                points = []
                for j in range(6):
                    if not ours:
                        start = (j * 6 + k) * 16
                        points.append(weighted(block(far, j * 6 + k, 16)[...], far, start + 8))
                    elif side:
                        index = axis * FACE + j * 6 + k
                        points.append(weighted(block(high, index, 16)[...], high, index * 16 + 8))
                    else:
                        n = node_of(axis, 0, j, k)
                        points.append(weighted(block(a_ref, n)[...], b_ref, (axis * NODES + n) * 8))
                table, offset, mid = (tab, M1, own_mid) if ours else (pair, 0, far_mid)
                for b in range(6):
                    for part in range(2):
                        total = None
                        for j in range(6):
                            term = row8(table, offset + b * 6 + j) * points[j][part]
                            total = term if total is None else total + term
                        block(mid, b * 6 + k, 16, 8 * part)[...] = total
            return carry

        def second(b, carry):
            for c in range(6):
                for part in range(2):
                    total = None
                    for k in range(6):
                        term = row8(tab, M2 + c * 6 + k) * block(own_mid, b * 6 + k, 16, 8 * part)[...]
                        term = term + row8(pair, 40 + c * 6 + k) * block(far_mid, b * 6 + k, 16, 8 * part)[...]
                        total = term if total is None else total + term
                    if side == 0:
                        place = block(acc, node_of(axis, 0, b, c), 16, 8 * part)
                        place[...] = place[...] + total
                    else:
                        for layer in range(1, 6):
                            place = block(acc, node_of(axis, layer, b, c), 16, 8 * part)
                            place[...] = place[...] + jnp.where(ob == float(layer), total, 0.0)
            return carry

        lax.fori_loop(0, 6, first, 0)
        lax.fori_loop(0, 6, second, 0)

    zero = jnp.zeros((8, SLOTS), jnp.float32)
    large = jnp.full((8, SLOTS), 1e30, jnp.float32)

    def reduce(t, carry):
        mean_a, mean_b, low_a, low_b = carry
        weight = row8(tab, W0 + t // 6) * row8(tab, W0 + t % 6)
        active = row8(tab, ACT + t // 6) * row8(tab, ACT + t % 6)
        for c in range(6):
            value_a = block(acc, t * 6 + c, 16)[...]
            value_b = block(acc, t * 6 + c, 16, 8)[...]
            here = weight * row8(tab, W0 + c)
            mask = active * row8(tab, ACT + c) > 0.0
            mean_a = mean_a + value_a * here
            mean_b = mean_b + value_b * here
            low_a = jnp.minimum(low_a, jnp.where(mask, value_a, 1e30))
            low_b = jnp.minimum(low_b, jnp.where(mask, value_b, 1e30))
        return mean_a, mean_b, low_a, low_b

    mean_a, mean_b, low_a, low_b = lax.fori_loop(0, FACE, reduce, (zero, zero, large, large))

    def limiter(mean, low):
        return jnp.minimum(
            1.0, jnp.maximum(mean - positivity_eps, 0.0) / jnp.maximum(mean - low, floor_gap)
        )

    scale_a, scale_b = limiter(mean_a, low_a), limiter(mean_b, low_b)
    is_species = iota((8, SLOTS), 0) == 0

    def write(t, carry):
        active = row8(tab, ACT + t // 6) * row8(tab, ACT + t % 6)
        for c in range(6):
            n = t * 6 + c
            value_a = block(acc, n, 16)[...]
            value_b = block(acc, n, 16, 8)[...]
            mask = active * row8(tab, ACT + c) > 0.0
            value_a = jnp.where(mask, mean_a + scale_a * (value_a - mean_a), 0.0)
            scaled = jnp.where(is_species, mean_b + scale_b * (value_b - mean_b), value_b)
            value_b = jnp.where(mask, scaled, 0.0)
            out[pl.ds(n, 8, stride=NODES), :] = value_a
            out[pl.ds(8 * NODES + n, 5, stride=NODES), :] = value_b[0:5, :]
        return carry

    lax.fori_loop(0, FACE, write, 0)


def finish(a, b, high, acc, tab, order, links, before, after, far_table):
    vmem = lambda rows: pltpu.VMEM((rows, SLOTS), jnp.float32)
    return pl.pallas_call(
        finish_body,
        out_shape=jax.ShapeDtypeStruct((NV * NODES, SLOTS), jnp.float32),
        scratch_shapes=[vmem(NODES * 16), vmem(FACE * 16), vmem(FACE * 16), vmem(FACE * 16), vmem(80)],
        name="finish",
    )(a, b, high, acc, tab, order, links, before, after, far_table)


def local(state_send, order_send, send_count, neighbours):
    peers = lax.axis_size(GROUP)
    own_table, far_table = element_tables()
    packed = pack(
        state_send.reshape(NV * NODES, SLOTS), order_send.reshape(1, SLOTS), send_count
    )
    blocks = packed.reshape(peers, SLOTS // peers * PITCH, 128)
    moved = lax.all_to_all(blocks, GROUP, split_axis=0, concat_axis=0, tiled=True)
    a, b, high, up, down, tab, order = prep(moved.reshape(SLOTS * PITCH, 128), own_table)
    devices = lax.axis_size(AXES)
    forward = [(i, i + 1) for i in range(devices - 1)]
    before = lax.ppermute(up, AXES, forward)
    after = lax.ppermute(down, AXES, [(j, i) for i, j in forward])
    acc = volume(a, b, tab)
    result = finish(a, b, high, acc, tab, order, neighbours, before, after, far_table)
    return result.reshape(NV, NODES, SLOTS)


def solution(mesh):
    placed = (
        P(None, None, AXES),
        P(AXES),
        P(AXES, None),
        P(None, AXES),
    )
    return jax.shard_map(
        local,
        mesh=mesh,
        in_specs=placed,
        out_specs=P(None, None, AXES),
        check_vma=False,
    )
```

time: 383 us -> 149 us (0.39); the launches traced: 378 us -> 149 us
  waiting for transfers between devices: 163 us -> 0.01 us
  local copies, waits for them, and re-layouts: 119 us -> 0.65 us
  blocking collectives: 0 us -> 103 us
  other arithmetic: 46.5 us -> 0 us
  Pallas kernels: 0 us -> 28 us
  starting transfers between devices: 44.7 us -> 17.6 us
    all_to_all x0 -> x1, blocking collectives: none -> 103 us  [local(): lax.all_to_all(blocks, GROUP, split_axis=0, concat_axis=0, tiled=True)]
    all_to_all x2 -> x0, waiting for transfers between devices: 100 us -> none  [the longest x1 89.4 us: local(): lax.all_to_all(state_send, ('gy', 'gz'), split_axis=2, concat_axis=2, til...]
    ppermute x2, waiting for transfers between devices: 62.9 us -> 0.01 us  [the longest x1 0.01 us: local(): before = lax.ppermute(up, AXES, forward)]
    gather x12 -> x0, local copies, waits for them, and re-layouts: 36.2 us -> none  [finish(): far_rows = jnp.take(extended[:, face ^ 1], links[face], axis=-1)]
    pallas_call x0 -> x4, Pallas kernels: none -> 28 us  [the longest x1 12.2 us: finish(): pl.pallas_call(finish_body, out_shape=jax.ShapeDtypeStruct((NV * NODES, S...]
    all_to_all x2 -> x0, starting transfers between devices: 27 us -> none  [the longest x1 20.3 us: local(): lax.all_to_all(order_tags, ('gy', 'gz'), split_axis=2, concat_axis=2, til...]
    squeeze x8 -> x0, local copies, waits for them, and re-layouts: 20.3 us -> none  [the longest x7 20.2 us: finish(): far_rows = jnp.take(extended[:, face ^ 1], links[face], axis=-1)]
    unnamed x322 -> x4, local copies, waits for them, and re-layouts: 19.7 us -> 0.65 us
  transfers between devices with their start and end apart: 4 -> 2, of which waited for: 3 -> 0; matrix products, arithmetic and copies ran while one was open for 9% -> 0% of each run, Pallas kernels for 0% -> 5%
where the time goes in v1:
time: 149 us
  blocking collectives  103 us (69%)
  Pallas kernels  28 us (19%)
  starting transfers between devices  17.6 us (12%)
    all_to_all x1, blocking collectives, local(): lax.all_to_all(blocks, GROUP, split_axis=0, concat_axis=0, tiled=True)  103 us
    ppermute x1, starting transfers between devices, local(): after = lax.ppermute(down, AXES, [(j, i) for i, j in forward])  15.2 us
    pallas_call x1, Pallas kernels, finish(): pl.pallas_call(finish_body, out_shape=jax.ShapeDtypeStruct((NV * NODES, S...  12.2 us
    pallas_call x1, Pallas kernels, volume(): pl.pallas_call(volume_body, out_shape=jax.ShapeDtypeStruct((NODES * 16, S...  7.03 us
    pallas_call x1, Pallas kernels, prep(): pl.pallas_call(prep_body, out_shape=(shape(NODES * 8), shape(3 * NODES *...  5.67 us
    pallas_call x1, Pallas kernels, pack(): pl.pallas_call(lambda *refs: pack_body(peers, *refs), out_shape=jax.Shape...  3.14 us
  transfers between devices with their start and end apart: 2, of which 0 were waited for; matrix products, arithmetic and copies ran while one was open for 0% of the time, Pallas kernels for 5%

profile of v1, /device:TPU:32, one launch (start us, length us, event | category | flops | bytes accessed | tf_op | source)
XLA Modules:
  0.0 149.2 jit_solution(16348590607749976055)
XLA Ops:
  0.0 3.1 %pack.1 = f32[3072,128]{1,0:T(8,128)} custom-call(f32[2808,128]{1,0:T(8,128)} %bitcast.7, s32[1,128]{1,0:T(1,128)} %bitcast.8, s32[1,64]{1,0:T(1,128)} %refs_2_.1), custom_call_target="tpu_custom_call" | custom-call | tf_op jit(solution)/shard_map/pack/pallas_call | solution.py:160
  3.1 102.9 %all_to_all.5 = f32[64,48,128]{2,1,0:T(8,128)} all-to-all(f32[64,48,128]{2,1,0:T(8,128)} %bitcast.6), channel_id=1, replica_groups=mesh['gx'=8,'gy'=8,'gz'=8] {'gy','gz'}, dimensions={0} | all-to-all | bytes 3145728 | tf_op jit(solution)/shard_map/all_to_all | solution.py:489
  106.0 5.7 %prep.1 = (f32[1728,128]{1,0:T(8,128)}, f32[5184,128]{1,0:T(8,128)}, f32[1728,128]{1,0:T(8,128)}, f32[224,128]{1,0:T(8,128)}, f32[224,128]{1,0:T(8,128)}, /*index=5*/f32[136,128]{1,0:T(8,128)}, f32[8,128]{1,0:T(8,128)}) custom-call(f32[3072,128]{1,0:T(8,128)} %bitcast.5, f32[136,128]{1,0:T(8,128)} %constant.4.clone.own_table), custom_call_target="tpu_custom_call" | custom-call | tf_op jit(solution)/shard_map/prep/pallas_call | solution.py:248
  111.7 2.4 %collective-permute-start = (f32[224,128]{1,0:T(8,128)}, f32[224,128]{1,0:T(8,128)S(1)}, u32[]{:S(2)}, u32[]{:S(2)}) collective-permute-start(f32[224,128]{1,0:T(8,128)} %get-tuple-element.17), channel_id=1, source_target_pairs={{0,1},{1,2},{2,3},{3,4},{4,5},{5,6},{6,7},{7,8},{8,9},{9,10},{10,1... | collective-permute-start | bytes 344072 | tf_op jit(solution)/shard_map/ppermute | solution.py:493
  114.1 15.2 %collective-permute-start.1 = (f32[224,128]{1,0:T(8,128)}, f32[224,128]{1,0:T(8,128)S(1)}, u32[]{:S(2)}, u32[]{:S(2)}) collective-permute-start(f32[224,128]{1,0:T(8,128)} %get-tuple-element.18), channel_id=1, source_target_pairs={{1,0},{2,1},{3,2},{4,3},{5,4},{6,5},{7,6},{8,7},{9,8},{10,9},{11,1... | collective-permute-start | bytes 344072 | tf_op jit(solution)/shard_map/ppermute | solution.py:494
  129.3 7.0 %volume.1.acc_in = f32[3456,128]{1,0:T(8,128)} custom-call(f32[1728,128]{1,0:T(8,128)} %get-tuple-element.12.a_ref, f32[5184,128]{1,0:T(8,128)} %get-tuple-element.13.b_ref, f32[136,128]{1,0:T(8,128)} %get-tuple-element.15.tab), custom_call_target="tpu_custom_call" | custom-call | tf_op jit(solution)/shard_map/volume/pallas_call | solution.py:310
  136.3 0.0 collective-permute-done.before
  136.3 0.0 copy-start
  136.3 0.0 collective-permute-done.1.after
  136.3 0.0 copy-start.1
  136.3 0.6 copy-done
  137.0 0.0 copy-done.1
  137.0 12.2 %finish.1 = f32[2808,128]{1,0:T(8,128)} custom-call(f32[1728,128]{1,0:T(8,128)} %get-tuple-element.12.a_ref, f32[5184,128]{1,0:T(8,128)} %get-tuple-element.13.b_ref, f32[1728,128]{1,0:T(8,128)} %get-tuple-element.14.high, f32[3456,128]{1,0:T(8,128)} %volume.1.acc_in, f32[136,128]{1,0:T(8,128)} %get-tuple-element.15.tab, f32[8,128]{1,0:T(8,128)} %get-tuple-element.16.order, ...), custom_call_target="tpu_custom_call" | custom-call | tf_op jit(solution)/shard_map/finish/pallas_call | solution.py:474
Async XLA Ops:
  111.7 24.6 %collective-permute-start = (f32[224,128]{1,0:T(8,128)}, f32[224,128]{1,0:T(8,128)S(1)}, u32[]{:S(2)}, u32[]{:S(2)}) collective-permute-start(f32[224,128]{1,0:T(8,128)} %get-tuple-element.17), channel_id=1, source_target_pairs={{0,1},{1,2},{2,3},{3,4},{4,5},{5,6},{6,7},{7,8},{8,9},{9,10},{10,1... | collective-permute-start | bytes 344072 | tf_op jit(solution)/shard_map/ppermute | solution.py:493
  114.1 22.3 %collective-permute-start.1 = (f32[224,128]{1,0:T(8,128)}, f32[224,128]{1,0:T(8,128)S(1)}, u32[]{:S(2)}, u32[]{:S(2)}) collective-permute-start(f32[224,128]{1,0:T(8,128)} %get-tuple-element.18), channel_id=1, source_target_pairs={{1,0},{2,1},{3,2},{4,3},{5,4},{6,5},{7,6},{8,7},{9,8},{10,9},{11,1... | collective-permute-start | bytes 344072 | tf_op jit(solution)/shard_map/ppermute | solution.py:494
  136.3 0.6 copy-start
  136.3 0.7 copy-start.1

commit v2 on v1

--- a/solution.py
+++ b/solution.py
@@ -4,7 +4,8 @@
 from jax import lax
 from jax.experimental import pallas as pl
 from jax.experimental.pallas import tpu as pltpu
-from jax.sharding import PartitionSpec as P
+from jax.sharding import Mesh, PartitionSpec as P
+
 
 NV = 13
 PMAX = 5
@@ -17,13 +18,18 @@
 PITCH = 24
 FEATS = ROWS * 128
 HALO = 216
+HALF = SLOTS // 2
+HEAD = 8
+ROOM = 584
+FLAG = 22
 
 step_scale = 0.02
 positivity_eps = 0.001
 floor_gap = 0.05
 
-AXES = ("gx", "gy", "gz")
-GROUP = ("gy", "gz")
+AXES = ("gx", "y", "zh", "gz")
+GROUP = ("y", "zh", "gz")
+SIDE = ("y", "gz")
 D0, M1, M2, W0, ACT, OWN_ROWS = 0, 40, 80, 120, 128, 136
 
 
@@ -140,14 +146,17 @@
     return ref.at[pl.ds(start, 8), :]
 
 
-def pack_body(peers, state, order, count, out, feats):
+def slot_tags(peers, order, count):
     capacity = SLOTS // peers
     spread = (iota((peers, SLOTS), 1) // capacity == iota((peers, SLOTS), 0)).astype(jnp.float32)
     counts = jnp.broadcast_to(count[...].astype(jnp.float32), (8, peers))
     per_slot = jnp.dot(counts, spread, preferred_element_type=jnp.float32)
     place = (iota((8, SLOTS), 1) % capacity).astype(jnp.float32)
     orders = jnp.broadcast_to(order[...].astype(jnp.float32), (8, SLOTS))
-    tag = jnp.where(place < per_slot, orders, 0.0)
+    return jnp.where(place < per_slot, orders, 0.0)
+
+
+def transpose_elements(state, tag, out, feats):
     for n in range(NODES):
         feats[pl.ds(RANK[n] * NV, NV), :] = state[pl.ds(n, NV, stride=NODES), :]
     feats[pl.ds(NODES * NV, 8), :] = tag
@@ -155,17 +164,111 @@
         out[pl.ds(k, SLOTS, stride=PITCH), :] = feats[pl.ds(k * 128, 128), :].T
 
 
-def pack(state, order, count):
+def pack_all_body(peers, state, order, count, out, feats):
+    transpose_elements(state, slot_tags(peers, order, count), out, feats)
+
+
+def pack_all(state, order, count):
     peers = count.shape[-1]
     return pl.pallas_call(
-        lambda *refs: pack_body(peers, *refs),
+        lambda *refs: pack_all_body(peers, *refs),
         out_shape=jax.ShapeDtypeStruct((SLOTS * PITCH, 128), jnp.float32),
         scratch_shapes=[pltpu.VMEM((FEATS, SLOTS), jnp.float32)],
+        name="pack_all",
+    )(state, order, count)
+
+
+def rows_of(order):
+    rows = jnp.where(order == 5, 22, jnp.where(order == 4, 13, 7))
+    return jnp.where(order == 3, rows, jnp.where(order == 2, 3, jnp.where(order == 1, 1, jnp.where(order == 0, 0, rows))))
+
+
+def pack_body(peers, chunk, side, order_s, count_s, state, order, count, own, away, feats, rows, room):
+    capacity = SLOTS // peers
+    tag = slot_tags(peers, order, count)
+    transpose_elements(state, tag, rows, feats)
+    zh = side[0]
+
+    def send(e, total):
+        slot = (e // chunk) * (2 * chunk) + (1 - zh) * chunk + e % chunk
+        alive = slot % capacity < count_s[slot // capacity]
+        used = jnp.where(alive, rows_of(order_s[slot]), 0)
+        offset = jnp.minimum(total, ROOM)
+        room[pl.ds(offset, PITCH), :] = rows[pl.ds(pl.multiple_of(slot * PITCH, 8), PITCH), :]
+        return total + used
+
+    total = lax.fori_loop(0, HALF, send, jnp.int32(0))
+    away[pl.ds(0, HEAD), :] = tag
+    away[pl.ds(HEAD, ROOM), :] = room[pl.ds(0, ROOM), :]
+    flag = jnp.full((1, 128), jnp.where(total > ROOM, 1.0, 0.0), jnp.float32)
+    for y in range(HALF // chunk):
+        start = pl.multiple_of((2 * chunk * y + chunk * zh) * PITCH, 8)
+        own[pl.ds(y * chunk * PITCH, chunk * PITCH), :] = rows[pl.ds(start, chunk * PITCH), :]
+    for e in range(0, HALF, capacity):
+        own[pl.ds(e * PITCH + FLAG, 1), :] = flag
+
+
+def pack(state, order, count, side, chunk):
+    peers = count.shape[-1]
+    vmem = lambda rows: pltpu.VMEM((rows, 128), jnp.float32)
+    whole = pl.BlockSpec(memory_space=pltpu.VMEM)
+    scalar = pl.BlockSpec(memory_space=pltpu.SMEM)
+    return pl.pallas_call(
+        lambda *refs: pack_body(peers, chunk, *refs),
+        in_specs=[scalar, scalar, scalar, whole, whole, whole],
+        out_shape=(
+            jax.ShapeDtypeStruct((HALF * PITCH, 128), jnp.float32),
+            jax.ShapeDtypeStruct((HEAD + ROOM, 128), jnp.float32),
+        ),
+        scratch_shapes=[vmem(FEATS), vmem(SLOTS * PITCH), vmem(ROOM + PITCH)],
         name="pack",
-    )(state, order, count)
-
-
-def prep_body(recv, own_table, a_ref, b_ref, high, up, down, tab, order, feats):
+    )(side, order, count.reshape(peers), state, order.reshape(1, SLOTS), count)
+
+
+def unpack_body(capacity, chunk, side, tags, came, out, room):
+    zh = side[0]
+    room[pl.ds(0, ROOM), :] = came[pl.ds(HEAD, ROOM), :]
+    lane = iota((1, 128), 1)
+
+    def take(e, total):
+        slot = (e // chunk) * (2 * chunk) + zh * chunk + e % chunk
+        order = tags[0, slot]
+        offset = jnp.minimum(total, ROOM)
+        start = pl.multiple_of(e * PITCH, 8)
+        out[pl.ds(start, PITCH), :] = room[pl.ds(offset, PITCH), :]
+        last = out[pl.ds(start + ROWS - 1, 1), :]
+        out[pl.ds(start + ROWS - 1, 1), :] = jnp.where(lane >= 120, order, last)
+        return total + rows_of(order)
+
+    total = lax.fori_loop(0, HALF, take, jnp.int32(0))
+    flag = jnp.full((1, 128), jnp.where(total > ROOM, 1.0, 0.0), jnp.float32)
+    for e in range(0, HALF, capacity):
+        out[pl.ds(e * PITCH + FLAG, 1), :] = flag
+
+
+def unpack(came, side, capacity, chunk):
+    return pl.pallas_call(
+        lambda *refs: unpack_body(capacity, chunk, *refs),
+        grid=(1,),
+        in_specs=[
+            pl.BlockSpec(memory_space=pltpu.SMEM),
+            pl.BlockSpec((HEAD, 128), lambda i: (0, 0), memory_space=pltpu.SMEM),
+            pl.BlockSpec((HEAD + ROOM, 128), lambda i: (0, 0)),
+        ],
+        out_specs=pl.BlockSpec((HALF * PITCH, 128), lambda i: (0, 0)),
+        out_shape=jax.ShapeDtypeStruct((HALF * PITCH, 128), jnp.float32),
+        scratch_shapes=[pltpu.VMEM((ROOM + PITCH, 128), jnp.float32)],
+        name="unpack",
+    )(side, came, came)
+
+
+def prep_body(chunk, side, near, away, own_table, a_ref, b_ref, high, up, down, tab, order, feats, recv):
+    zh = side[0]
+    for y in range(HALF // chunk):
+        size = chunk * PITCH
+        for source, half in ((near, zh), (away, 1 - zh)):
+            start = pl.multiple_of((2 * chunk * y + chunk * half) * PITCH, 8)
+            recv[pl.ds(start, size), :] = source[pl.ds(y * size, size), :]
     for k in range(ROWS):
         feats[pl.ds(k * 128, 128), :] = recv[pl.ds(k, SLOTS, stride=PITCH), :].T
     ob = row8(feats, NODES * NV)
@@ -243,10 +346,12 @@
     down[pl.ds(HALO, 8), :] = ob
 
 
-def prep(recv, own_table):
+def prep(near, away, own_table, side, chunk):
+    whole = pl.BlockSpec(memory_space=pltpu.VMEM)
     shape = lambda rows: jax.ShapeDtypeStruct((rows, SLOTS), jnp.float32)
     return pl.pallas_call(
-        prep_body,
+        lambda *refs: prep_body(chunk, *refs),
+        in_specs=[pl.BlockSpec(memory_space=pltpu.SMEM), whole, whole, whole],
         out_shape=(
             shape(NODES * 8),
             shape(3 * NODES * 8),
@@ -256,9 +361,12 @@
             shape(OWN_ROWS),
             shape(8),
         ),
-        scratch_shapes=[pltpu.VMEM((FEATS, SLOTS), jnp.float32)],
+        scratch_shapes=[
+            pltpu.VMEM((FEATS, SLOTS), jnp.float32),
+            pltpu.VMEM((SLOTS * PITCH, 128), jnp.float32),
+        ],
         name="prep",
-    )(recv, own_table)
+    )(side, near, away, own_table)
 
 
 def flux_rows(axis, scale):
@@ -481,13 +589,43 @@
 
 def local(state_send, order_send, send_count, neighbours):
     peers = lax.axis_size(GROUP)
+    capacity = SLOTS // peers
+    chunk = capacity * lax.axis_size("gz")
     own_table, far_table = element_tables()
-    packed = pack(
-        state_send.reshape(NV * NODES, SLOTS), order_send.reshape(1, SLOTS), send_count
+    state = state_send.reshape(NV * NODES, SLOTS)
+    side = lax.axis_index("zh").reshape(1)
+    own, away = pack(state, order_send, send_count, side, chunk)
+    came = lax.ppermute(away, "zh", [(0, 1), (1, 0)])
+
+    def spread(half):
+        blocks = half.reshape(peers // 2, capacity * PITCH, 128)
+        return lax.all_to_all(blocks, SIDE, split_axis=0, concat_axis=0, tiled=True)
+
+    near_blocks = spread(own)
+    away_blocks = spread(unpack(came, side, capacity, chunk))
+    full = jnp.maximum(jnp.max(near_blocks[:, FLAG, 0]), jnp.max(away_blocks[:, FLAG, 0])) > 0.0
+
+    def direct():
+        packed = pack_all(state, order_send.reshape(1, SLOTS), send_count)
+        blocks = packed.reshape(peers, capacity * PITCH, 128)
+        moved = lax.all_to_all(blocks, GROUP, split_axis=0, concat_axis=0, tiled=True)
+        moved = moved.reshape(
+            lax.axis_size("y"), 2, lax.axis_size("gz"), capacity * PITCH, 128
+        )
+        halves = [
+            lax.dynamic_index_in_dim(moved, which, 1, keepdims=False).reshape(near_blocks.shape)
+            for which in (side[0], 1 - side[0])
+        ]
+        return halves[0], halves[1]
+
+    near_blocks, away_blocks = lax.cond(full, direct, lambda: (near_blocks, away_blocks))
+    a, b, high, up, down, tab, order = prep(
+        near_blocks.reshape(HALF * PITCH, 128),
+        away_blocks.reshape(HALF * PITCH, 128),
+        own_table,
+        side,
+        chunk,
     )
-    blocks = packed.reshape(peers, SLOTS // peers * PITCH, 128)
-    moved = lax.all_to_all(blocks, GROUP, split_axis=0, concat_axis=0, tiled=True)
-    a, b, high, up, down, tab, order = prep(moved.reshape(SLOTS * PITCH, 128), own_table)
     devices = lax.axis_size(AXES)
     forward = [(i, i + 1) for i in range(devices - 1)]
     before = lax.ppermute(up, AXES, forward)
@@ -498,6 +636,8 @@
 
 
 def solution(mesh):
+    sizes = mesh.devices.shape
+    parts = Mesh(mesh.devices.reshape(sizes[0], sizes[1] // 2, 2, sizes[2]), AXES)
     placed = (
         P(None, None, AXES),
         P(AXES),
@@ -506,7 +646,7 @@
     )
     return jax.shard_map(
         local,
-        mesh=mesh,
+        mesh=parts,
         in_specs=placed,
         out_specs=P(None, None, AXES),
         check_vma=False,

time: 149 us -> 134 us (0.90)
  the two profiles are of different devices: /device:TPU:32 before, /device:TPU:39 now
where the time goes in v2:
time: 134 us; the launch traced here: 133 us
  waiting for transfers between devices  47.8 us (36%)
  starting transfers between devices  47 us (35%)
  Pallas kernels  32.5 us (24%)
  other arithmetic  3.1 us (2%)
  local copies, waits for them, and re-layouts  1.4 us (1%)
  between operations  1.39 us (1%)
    ppermute x1, waiting for transfers between devices, local(): came = lax.ppermute(away, 'zh', [(0, 1), (1, 0)])  25.8 us
    all_to_all x2, starting transfers between devices, spread(): return lax.all_to_all(blocks, SIDE, split_axis=0, concat_axis=0, tiled=True)  17 us
    ppermute x1, starting transfers between devices, local(): came = lax.ppermute(away, 'zh', [(0, 1), (1, 0)])  14.7 us
    ppermute x1, starting transfers between devices, local(): before = lax.ppermute(up, AXES, forward)  13.4 us
    pallas_call x1, Pallas kernels, finish(): pl.pallas_call(finish_body, out_shape=jax.ShapeDtypeStruct((NV * NODES, S...  12.2 us
    all_to_all x2, waiting for transfers between devices, spread(): return lax.all_to_all(blocks, SIDE, split_axis=0, concat_axis=0, tiled=True)  11.6 us
    ppermute x1, waiting for transfers between devices, local(): after = lax.ppermute(down, AXES, [(j, i) for i, j in forward])  10.5 us
    pallas_call x1, Pallas kernels, volume(): pl.pallas_call(volume_body, out_shape=jax.ShapeDtypeStruct((NODES * 16, S...  7 us
  transfers between devices with their start and end apart: 5, of which 3 were waited for; matrix products, arithmetic and copies ran while one was open for 1% of the time, Pallas kernels for 8%

profile of v2, /device:TPU:39, one launch (start us, length us, event | category | flops | bytes accessed | tf_op | source)
XLA Modules:
  0.0 133.3 jit_solution(5499710713922417435)
XLA Ops:
  0.0 4.5 %pack.1 = (f32[1536,128]{1,0:T(8,128)}, f32[592,128]{1,0:T(8,128)}) custom-call(s32[1]{0:T(128)} %bitcast.7.refs_0_, s32[128]{0:T(128)} %refs_1_.1, s32[64]{0:T(128)} %bitcast.26, f32[2808,128]{1,0:T(8,128)} %bitcast.20, s32[1,128]{1,0:T(1,128)} %bitcast.24, s32[1,64]{1,0:T(1,128)} %refs_5_.1), custom_call_target="tpu_custom_call" | custom-call | tf_op jit(solution)/shard_map/pack/pallas_call | solution.py:216
  4.5 0.0 copy-start.6
  4.5 8.0 %all-to-all-start.1 = ((f32[32,48,128]{2,1,0:T(8,128)}), f32[32,48,128]{2,1,0:T(8,128)}, u32[]{:S(2)}, u32[]{:S(2)}) async-start(f32[32,48,128]{2,1,0:T(8,128)} %bitcast.23), calls=%async_computation.1 | async-start | bytes 1572864 | tf_op jit(solution)/shard_map/all_to_all | solution.py:602
  12.5 0.0 copy-start
  12.6 0.0 copy-start.4
  12.6 0.0 copy-start.5
  12.6 0.0 copy-done.6
  12.6 14.7 %collective-permute-start = (f32[592,128]{1,0:T(8,128)S(1)}, f32[592,128]{1,0:T(8,128)S(1)}, u32[]{:S(2)}, u32[]{:S(2)}) collective-permute-start(f32[592,128]{1,0:T(8,128)S(1)} %copy-done.6), channel_id=1, source_target_pairs={{0,8},{8,0},{1,9},{9,1},{2,10},{10,2},{3,11},{11,3},{4,12},{12,4},... | collective-permute-start | bytes 909320 | tf_op jit(solution)/shard_map/ppermute | solution.py:598
  27.3 25.8 %collective-permute-done.refs_1_.refs_2_ = f32[592,128]{1,0:T(8,128)S(1)} collective-permute-done((f32[592,128]{1,0:T(8,128)S(1)}, f32[592,128]{1,0:T(8,128)S(1)}, u32[]{:S(2)}, u32[]{:S(2)}) %collective-permute-start) | collective-permute-done | bytes 303136 | tf_op jit(solution)/shard_map/ppermute | solution.py:598
  53.1 0.0 copy-start.1
  53.1 0.7 copy-done.1
  53.8 3.1 %unpack.1 = f32[1536,128]{1,0:T(8,128)} custom-call(s32[1]{0:T(128)} %bitcast.7.refs_0_, f32[592,128]{1,0:T(8,128)} %copy-done.1, f32[592,128]{1,0:T(8,128)} %copy-done.1), custom_call_target="tpu_custom_call" | custom-call | tf_op jit(solution)/shard_map/unpack/pallas_call | solution.py:250
  56.9 0.0 all-to-all-done.1
  56.9 9.0 %all-to-all-start.2 = ((f32[32,48,128]{2,1,0:T(8,128)}), f32[32,48,128]{2,1,0:T(8,128)}, u32[]{:S(2)}, u32[]{:S(2)}) async-start(f32[32,48,128]{2,1,0:T(8,128)} %bitcast.22), calls=%async_computation.2 | async-start | bytes 1572864 | tf_op jit(solution)/shard_map/all_to_all | solution.py:602
  65.9 1.5 %slice_reduce_fusion.1 = f32[]{:T(128)} fusion(f32[32,48,128]{2,1,0:T(8,128)} %all-to-all-done.1), kind=kLoop, calls=%fused_computation.3 | loop fusion | flops 31 | bytes 132 | tf_op jit(solution)/shard_map/reduce_max | solution.py:606
  67.5 11.6 %all-to-all-done.2 = f32[32,48,128]{2,1,0:T(8,128)} async-done(((f32[32,48,128]{2,1,0:T(8,128)}), f32[32,48,128]{2,1,0:T(8,128)}, u32[]{:S(2)}, u32[]{:S(2)}) %all-to-all-start.2) | async-done | bytes 786464 | tf_op jit(solution)/shard_map/all_to_all | solution.py:602
  79.0 1.6 %slice_reduce_fusion = f32[]{:T(128)} fusion(f32[32,48,128]{2,1,0:T(8,128)} %all-to-all-done.2), kind=kLoop, calls=%fused_computation.2 | loop fusion | flops 31 | bytes 132 | tf_op jit(solution)/shard_map/reduce_max | solution.py:606
  81.9 0.0 copy-done
  81.9 0.0 copy-done.4
  81.9 0.0 copy-done.5
  81.9 5.8 %prep.1 = (f32[1728,128]{1,0:T(8,128)}, f32[5184,128]{1,0:T(8,128)}, f32[1728,128]{1,0:T(8,128)}, f32[224,128]{1,0:T(8,128)}, f32[224,128]{1,0:T(8,128)}, /*index=5*/f32[136,128]{1,0:T(8,128)}, f32[8,128]{1,0:T(8,128)}) custom-call(s32[1]{0:T(128)} %bitcast.7.refs_0_, f32[1536,128]{1,0:T(8,128)} %get-tuple-element.40.refs_1_, ...), custom_call_target="tpu_custom_call" | custom-call | tf_op jit(solution)/shard_map/prep/pallas_call | solution.py:352
  87.7 13.4 %collective-permute-start.1 = (f32[224,128]{1,0:T(8,128)}, f32[224,128]{1,0:T(8,128)S(1)}, u32[]{:S(2)}, u32[]{:S(2)}) collective-permute-start(f32[224,128]{1,0:T(8,128)} %get-tuple-element.47), channel_id=1, source_target_pairs={{0,1},{1,2},{2,3},{3,4},{4,5},{5,6},{6,7},{7,8},{8,9},{9,10},{10,1... | collective-permute-start | bytes 344072 | tf_op jit(solution)/shard_map/ppermute | solution.py:631
  101.1 1.9 %collective-permute-start.2 = (f32[224,128]{1,0:T(8,128)}, f32[224,128]{1,0:T(8,128)S(1)}, u32[]{:S(2)}, u32[]{:S(2)}) collective-permute-start(f32[224,128]{1,0:T(8,128)} %get-tuple-element.48), channel_id=1, source_target_pairs={{1,0},{2,1},{3,2},{4,3},{5,4},{6,5},{7,6},{8,7},{9,8},{10,9},{11,1... | collective-permute-start | bytes 344072 | tf_op jit(solution)/shard_map/ppermute | solution.py:632
  103.0 7.0 %volume.1.acc_in = f32[3456,128]{1,0:T(8,128)} custom-call(f32[1728,128]{1,0:T(8,128)} %get-tuple-element.42.a_ref, f32[5184,128]{1,0:T(8,128)} %get-tuple-element.43.b_ref, f32[136,128]{1,0:T(8,128)} %get-tuple-element.45.tab), custom_call_target="tpu_custom_call" | custom-call | tf_op jit(solution)/shard_map/volume/pallas_call | solution.py:418
  110.0 0.0 collective-permute-done.1.before
  110.0 0.0 copy-start.2
  110.0 10.5 %collective-permute-done.2.after = f32[224,128]{1,0:T(8,128)S(1)} collective-permute-done((f32[224,128]{1,0:T(8,128)}, f32[224,128]{1,0:T(8,128)S(1)}, u32[]{:S(2)}, u32[]{:S(2)}) %collective-permute-start.2) | collective-permute-done | bytes 114720 | tf_op jit(solution)/shard_map/ppermute | solution.py:632
  120.5 0.0 copy-start.3
  120.5 0.0 copy-done.2
  120.5 0.6 copy-done.3
  121.1 12.2 %finish.1 = f32[2808,128]{1,0:T(8,128)} custom-call(f32[1728,128]{1,0:T(8,128)} %get-tuple-element.42.a_ref, f32[5184,128]{1,0:T(8,128)} %get-tuple-element.43.b_ref, f32[1728,128]{1,0:T(8,128)} %get-tuple-element.44.high, f32[3456,128]{1,0:T(8,128)} %volume.1.acc_in, f32[136,128]{1,0:T(8,128)} %get-tuple-element.45.tab, f32[8,128]{1,0:T(8,128)} %get-tuple-element.46.order, ...), custom_call_target="tpu_custom_call" | custom-call | tf_op jit(solution)/shard_map/finish/pallas_call | solution.py:582
  (1 shorter events, 0.0 us)
Async XLA Ops:
  4.5 8.1 %copy-start.6 = (f32[592,128]{1,0:T(8,128)S(1)}, f32[592,128]{1,0:T(8,128)}, u32[]{:S(2)}) copy-start(f32[592,128]{1,0:T(8,128)} %get-tuple-element.39) | copy-start | bytes 909316
  4.5 52.4 %all-to-all-start.1 = ((f32[32,48,128]{2,1,0:T(8,128)}), f32[32,48,128]{2,1,0:T(8,128)}, u32[]{:S(2)}, u32[]{:S(2)}) async-start(f32[32,48,128]{2,1,0:T(8,128)} %bitcast.23), calls=%async_computation.1 | async-start | bytes 1572864 | tf_op jit(solution)/shard_map/all_to_all | solution.py:602
  12.5 69.3 %copy-start = (f32[13,216,128]{2,1,0:T(8,128)S(1)}, f32[13,216,128]{2,1,0:T(8,128)}, u32[]{:S(2)}) copy-start(f32[13,216,128]{2,1,0:T(8,128)} %param.8) | copy-start | bytes 4313092
  12.6 69.3 %copy-start.4 = (s32[128]{0:T(128)S(1)}, s32[128]{0:T(128)}, u32[]{:S(2)}) copy-start(s32[128]{0:T(128)} %refs_1_.1) | copy-start | bytes 1540
  12.6 69.3 %copy-start.5 = (s32[1,64]{1,0:T(1,128)S(1)}, s32[1,64]{1,0:T(1,128)}, u32[]{:S(2)}) copy-start(s32[1,64]{1,0:T(1,128)} %refs_5_.1) | copy-start | bytes 772
  12.6 40.5 %collective-permute-start = (f32[592,128]{1,0:T(8,128)S(1)}, f32[592,128]{1,0:T(8,128)S(1)}, u32[]{:S(2)}, u32[]{:S(2)}) collective-permute-start(f32[592,128]{1,0:T(8,128)S(1)} %copy-done.6), channel_id=1, source_target_pairs={{0,8},{8,0},{1,9},{9,1},{2,10},{10,2},{3,11},{11,3},{4,12},{12,4},... | collective-permute-start | bytes 909320 | tf_op jit(solution)/shard_map/ppermute | solution.py:598
  53.1 0.7 copy-start.1
  56.9 22.1 %all-to-all-start.2 = ((f32[32,48,128]{2,1,0:T(8,128)}), f32[32,48,128]{2,1,0:T(8,128)}, u32[]{:S(2)}, u32[]{:S(2)}) async-start(f32[32,48,128]{2,1,0:T(8,128)} %bitcast.22), calls=%async_computation.2 | async-start | bytes 1572864 | tf_op jit(solution)/shard_map/all_to_all | solution.py:602
  87.7 22.3 %collective-permute-start.1 = (f32[224,128]{1,0:T(8,128)}, f32[224,128]{1,0:T(8,128)S(1)}, u32[]{:S(2)}, u32[]{:S(2)}) collective-permute-start(f32[224,128]{1,0:T(8,128)} %get-tuple-element.47), channel_id=1, source_target_pairs={{0,1},{1,2},{2,3},{3,4},{4,5},{5,6},{6,7},{7,8},{8,9},{9,10},{10,1... | collective-permute-start | bytes 344072 | tf_op jit(solution)/shard_map/ppermute | solution.py:631
  101.1 19.4 %collective-permute-start.2 = (f32[224,128]{1,0:T(8,128)}, f32[224,128]{1,0:T(8,128)S(1)}, u32[]{:S(2)}, u32[]{:S(2)}) collective-permute-start(f32[224,128]{1,0:T(8,128)} %get-tuple-element.48), channel_id=1, source_target_pairs={{1,0},{2,1},{3,2},{4,3},{5,4},{6,5},{7,6},{8,7},{9,8},{10,9},{11,1... | collective-permute-start | bytes 344072 | tf_op jit(solution)/shard_map/ppermute | solution.py:632
  110.0 10.5 %copy-start.2 = (f32[224,128]{1,0:T(8,128)}, f32[224,128]{1,0:T(8,128)S(1)}, u32[]{:S(2)}) copy-start(f32[224,128]{1,0:T(8,128)S(1)} %collective-permute-done.1.before) | copy-start | bytes 344068
  120.5 0.7 copy-start.3
